TPU v7x, 256 devices: a whole 4x4x8 slice. The times are simulated.
256 devices in a mesh: exp: 32 (over y, z_hi, core), hid: 8 (over z_lo, x).
Axes of the slice: x: 4, y: 4, z: 8 (z_hi: 4, z_lo: 2; z = z_hi * 2 + z_lo), core: 2. Of those that a mesh axis runs over, the one named last changes fastest.
Arguments:
- tokens: bfloat16 [1024, 2048], P(('exp', 'hid')), may hold values from -6 to 6
- grad_out: bfloat16 [1024, 2048], P(('exp', 'hid')), may hold values from -3 to 3
- router_logits: float32 [1024, 128], P(('exp', 'hid')), may hold values from -12 to 330
- selected: int32 [1024, 8], P(('exp', 'hid')), may hold values from 0 to 127, as said below
- router_w: bfloat16 [2048, 128], replicated, may hold values from -0.59765625 to 0.59765625
- w_gate: bfloat16 [256, 2048, 384], P(('exp', 'hid')), may hold values from -0.125 to 0.125
- w_up: bfloat16 [256, 2048, 384], P(('exp', 'hid')), may hold values from -0.125 to 0.125
- w_down: bfloat16 [256, 384, 2048], P(('exp', 'hid')), may hold values from -0.21875 to 0.21875
Outputs:
- x_grad: bfloat16 [1024, 2048], P(('exp', 'hid'))
- router_grad: float32 [2048, 128], P(('exp', 'hid'))
Inputs may be any that keep to these rules, and one draw needn't show every extreme that they name: `selected`: each row names 8 different experts; within each aligned block of 32 rows (the tokens of one index of exp) no expert is named by more than 4 rows, and in every block some expert is named by exactly 4 rows.
All inputs are finite; a program needn't handle non-finite values.
Results may differ from a plain program's by a relative error of at most 0.0075.
Values may be sent and summed in bfloat16 or wider, within the bound.
A program may use at most 64 MiB of HBM per device.

v0:
```python
import jax
import jax.numpy as jnp
from jax import lax
from jax.sharding import PartitionSpec as P


def softmax_rows(values):
    top_val = jnp.max(values, axis=-1, keepdims=True)
    raised = jnp.exp(values - top_val)
    return raised / jnp.sum(raised, axis=-1, keepdims=True)


def combine_table(logits, chosen, expert_count):
    picked = jnp.take_along_axis(logits, chosen, axis=1)
    weights = softmax_rows(picked)
    expert_ids = jnp.arange(expert_count, dtype=jnp.int32)
    matched = (chosen[:, :, None] == expert_ids[None, None, :]).astype(jnp.float32)
    return jnp.sum(weights[:, :, None] * matched, axis=1).astype(jnp.bfloat16)


CAP = 4


def slot_rows(column, group_rows):
    shaped = column.reshape(column.shape[:-1] + (-1, group_rows))
    place = jnp.arange(group_rows, dtype=jnp.int32)
    key = jnp.where(shaped != 0, 2 * group_rows - place, -place)
    return lax.top_k(key, CAP)[1]


def dense_terms(x_rows, g_rows, w_gate, w_up, w_down):
    gate_pre = jnp.einsum("td,udf->utf", x_rows, w_gate, preferred_element_type=jnp.float32)
    up_pre = jnp.einsum("td,udf->utf", x_rows, w_up, preferred_element_type=jnp.float32)
    back_grad = jnp.einsum("td,ufd->utf", g_rows, w_down, preferred_element_type=jnp.float32)
    sig_gate = jax.nn.sigmoid(gate_pre)
    act_gate = gate_pre * sig_gate
    score_part = jnp.sum(act_gate * up_pre * back_grad, axis=2).T
    return (score_part, gate_pre, up_pre, back_grad)


def sparse_terms(gate_pre, up_pre, back_grad, column, w_gate, w_up, group_rows):
    picked = slot_rows(column, group_rows)
    groups = picked.shape[1]
    starts = (jnp.arange(groups, dtype=jnp.int32) * group_rows)[None, :, None]
    rows = (picked + starts).reshape(picked.shape[0], -1)
    take = lambda a: jnp.take_along_axis(a, rows[:, :, None], axis=1)
    gate_s, up_s, back_s = (take(gate_pre), take(up_pre), take(back_grad))
    col_s = jnp.take_along_axis(column, rows, axis=1)
    sig_gate = jax.nn.sigmoid(gate_s)
    act_gate = gate_s * sig_gate
    weighted = col_s[:, :, None] * back_s
    grad_gate = (weighted * up_s * sig_gate * (1.0 + gate_s * (1.0 - sig_gate))).astype(
        jnp.bfloat16
    )
    grad_up = (weighted * act_gate).astype(jnp.bfloat16)
    part = jnp.einsum("usf,udf->usd", grad_gate, w_gate, preferred_element_type=jnp.float32)
    part = part + jnp.einsum("usf,udf->usd", grad_up, w_up, preferred_element_type=jnp.float32)
    return part.reshape(part.shape[0], groups, CAP, part.shape[-1])


def on_device(tokens, grad_out, router_logits, selected, router_w, w_gate, w_up, w_down):
    tok_local, model_width = tokens.shape
    unit_count = w_gate.shape[0]
    expert_count = router_logits.shape[1]
    spread_exp = lax.axis_size("exp")
    spread_hid = lax.axis_size("hid")
    group_rows = spread_hid * tok_local
    own_exp = lax.axis_index("exp")
    own_hid = lax.axis_index("hid")
    own_block = lax.axis_index(("exp", "hid"))
    unit_expert = (own_block * unit_count + jnp.arange(unit_count, dtype=jnp.int32)) // 2
    expert_ids = jnp.arange(expert_count, dtype=jnp.int32)
    unit_pick = (expert_ids[:, None] == unit_expert[None, :]).astype(jnp.bfloat16)
    combine = combine_table(router_logits, selected, expert_count)
    packed = jnp.concatenate([tokens, grad_out, combine], axis=1)
    gathered = lax.all_gather(
        lax.all_gather(packed, "hid", axis=0, tiled=True), "exp", axis=0, tiled=True
    )
    combine_all = gathered[:, 2 * model_width :]
    score_part, gate_pre, up_pre, back_grad = dense_terms(
        gathered[:, :model_width], gathered[:, model_width : 2 * model_width], w_gate, w_up, w_down
    )
    column = jnp.dot(combine_all, unit_pick, preferred_element_type=jnp.float32).T
    part = sparse_terms(gate_pre, up_pre, back_grad, column, w_gate, w_up, group_rows)
    lane = 128
    score_grp = jnp.swapaxes(
        score_part.T.reshape(unit_count, spread_exp, CAP, group_rows // CAP), 0, 1
    )
    score_grp = jnp.pad(score_grp, ((0, 0), (0, 0), (0, 0), (0, lane - group_rows // CAP)))
    sent = jnp.concatenate([jnp.swapaxes(part, 0, 1), score_grp], axis=3)
    arrived_part = lax.all_to_all(sent, "exp", split_axis=0, concat_axis=0, tiled=True)
    sender_block = (jnp.arange(spread_exp, dtype=jnp.int32) * spread_hid + own_hid)[:, None]
    sender_expert = (
        sender_block * unit_count + jnp.arange(unit_count, dtype=jnp.int32)[None, :]
    ) // 2
    own_combine = lax.dynamic_slice_in_dim(combine_all, own_exp * group_rows, group_rows, 0)
    sender_pick = (expert_ids[:, None] == sender_expert.reshape(1, -1)).astype(jnp.bfloat16)
    sender_column = jnp.dot(own_combine, sender_pick, preferred_element_type=jnp.float32).T
    sender_rows = slot_rows(sender_column, group_rows).reshape(-1)
    place = (sender_rows[:, None] == jnp.arange(group_rows, dtype=jnp.int32)[None, :]).astype(
        jnp.float32
    )
    group_sum = jnp.einsum(
        "sj,sd->jd",
        place,
        arrived_part[..., :model_width].reshape(-1, model_width),
        precision=lax.Precision.HIGHEST,
        preferred_element_type=jnp.float32,
    )
    got_scores = arrived_part[..., model_width : model_width + group_rows // CAP]
    got_scores = got_scores.reshape(spread_exp, unit_count, spread_hid, tok_local)
    score_cols = spread_exp * unit_count
    score_width = -(-score_cols // lane) * lane
    hid_scores = jnp.transpose(got_scores, (2, 3, 0, 1)).reshape(spread_hid, tok_local, score_cols)
    hid_scores = jnp.pad(hid_scores, ((0, 0), (0, 0), (0, score_width - score_cols)))
    hid_sent = jnp.concatenate(
        [group_sum.reshape(spread_hid, tok_local, model_width), hid_scores], axis=2
    )
    spread_rows = lax.all_to_all(hid_sent, "hid", split_axis=0, concat_axis=0, tiled=True)
    input_sum = jnp.sum(spread_rows[..., :model_width], axis=0)
    own_scores = spread_rows[..., model_width : model_width + score_cols]
    own_scores = own_scores.reshape(spread_hid, tok_local, spread_exp, unit_count)
    unit_scores = jnp.transpose(own_scores, (1, 2, 0, 3)).reshape(tok_local, -1)
    expert_scores = jnp.sum(unit_scores.reshape(tok_local, expert_count, 2), axis=2)
    probs_all = softmax_rows(router_logits)
    mean_score = jnp.sum(probs_all * expert_scores, axis=1, keepdims=True)
    logit_grad = (probs_all * (expert_scores - mean_score)).astype(jnp.bfloat16)
    devices = spread_exp * spread_hid
    logit_all = lax.all_to_all(
        jnp.broadcast_to(logit_grad[None], (devices,) + logit_grad.shape),
        ("exp", "hid"),
        0,
        0,
        tiled=True,
    ).reshape(-1, expert_count)
    grad_rows = model_width // devices
    token_cols = lax.dynamic_slice_in_dim(gathered, own_block * grad_rows, grad_rows, 1)
    router_grad = jnp.einsum("tc,te->ce", token_cols, logit_all, preferred_element_type=jnp.float32)
    router_part = jnp.einsum("te,de->td", logit_grad, router_w, preferred_element_type=jnp.float32)
    x_grad = (input_sum + router_part).astype(jnp.bfloat16)
    return (x_grad, router_grad)


def solution(mesh):
    placed = (
        P(("exp", "hid"), None),
        P(("exp", "hid"), None),
        P(("exp", "hid"), None),
        P(("exp", "hid"), None),
        P(),
        P(("exp", "hid"), None, None),
        P(("exp", "hid"), None, None),
        P(("exp", "hid"), None, None),
    )
    return jax.shard_map(
        on_device,
        mesh=mesh,
        in_specs=placed,
        out_specs=(P(("exp", "hid"), None), P(("exp", "hid"), None)),
        check_vma=False,
    )
```

profile of v0, /device:TPU:1, one launch (start us, length us, event | category | flops | bytes accessed | tf_op | source)
XLA Modules:
  0.0 250.1 jit_solution(14854167661253626803)
XLA Ops:
  8.1 1.4 gather_fusion.1
  10.2 24.1 %all-gather = bf16[8,4,4224]{2,1,0:T(4,128)(2,1)S(1)} all-gather(bf16[1,4,4224]{2,1,0:T(4,128)(2,1)S(1)} %maximum_bitcast_fusion), channel_id=1, replica_groups=mesh['exp'=32,'hid'=8] {'hid'}, dimensions={0}, use_global_device_ids=true | all-gather | bytes 304128 | tf_op jit(solution)/shard_map/all_gather | solution.py:77
  35.1 85.0 %all-gather.3.cloned.1.call-done = bf16[1024,4224]{1,0:T(8,128)(2,1)} async-done(((bf16[32,4224]{1,0:T(8,128)(2,1)}), bf16[1024,4224]{1,0:T(8,128)(2,1)}) %all-gather.3.cloned.1.call-update) | async-done | bytes 8650768 | tf_op jit(solution)/shard_map/all_gather | solution.py:76
  123.3 1.5 gather_fusion
  124.8 5.3 %fusion.4 = f32[1024,384]{0,1:T(8,128)} fusion(bf16[1024,4224]{1,0:T(8,128)(2,1)} %all-gather.3.cloned.1.call-done, bf16[1,2048,384]{2,1,0:T(8,128)(2,1)S(1)} %copy-done.2), kind=kOutput, calls=%fused_computation.9 | convolution fusion | flops 1610612736 | bytes 7340032 | tf_op jit(solution)/shard_map/td,udf->utf/dot_general | solution.py:33
  130.0 1.9 copy.90
  131.9 5.2 %fusion.2 = f32[1024,384]{0,1:T(8,128)} fusion(bf16[1024,4224]{1,0:T(8,128)(2,1)} %all-gather.3.cloned.1.call-done, bf16[1,2048,384]{2,1,0:T(8,128)(2,1)S(1)} %copy-done), kind=kOutput, calls=%fused_computation.7 | convolution fusion | flops 1610612736 | bytes 7340032 | tf_op jit(solution)/shard_map/td,udf->utf/dot_general | solution.py:32
  137.1 3.1 %copy.91 = f32[1024,384]{1,0:T(8,128)} copy(f32[1024,384]{0,1:T(8,128)} %fusion.2) | data formatting | bytes 3145728 | tf_op jit(solution)/shard_map/jit(take_along_axis)/Arg_0.9 | solution.py:46
  140.2 1.4 gather_fusion.3
  141.6 2.4 gather_fusion.4
  144.0 6.2 %fusion.7 = (f32[1024]{0:T(1024)S(1)}, f32[1024,384]{0,1:T(8,128)}) fusion(f32[1024,384]{0,1:T(8,128)S(1)} %copy-done.4, f32[1024,384]{0,1:T(8,128)} %fusion.2, bf16[1,384,2048]{2,1,0:T(8,128)(2,1)} %param.17, bf16[1024,4224]{1,0:T(8,128)(2,1)} %all-gather.3.cloned.1.call-done), kind=kOutput, calls=%fused_computation.15 | convolution fusion | flops 1613364224 | bytes 10489856 | tf_op jit(solution)/shard_map/td,ufd->utf/dot_general | solution.py:34
  150.9 1.9 copy.89
  154.3 1.7 fusion.11
  156.7 1.3 transpose_reshape.6
  158.0 2.6 %pad_maximum_fusion = f32[32,1,4,2176]{3,2,1,0:T(4,128)} fusion(f32[32,1,4,128]{3,2,1,0:T(4,128)S(1)} %copy-done.6, f32[32,1,4,2048]{3,2,1,0:T(4,128)} %bitcast.146), kind=kLoop, calls=%fused_computation.28 | loop fusion | flops 278528 | bytes 2228224 | tf_op jit(solution)/shard_map/concatenate | solution.py:90
  160.5 10.4 %all-to-all-start = ((f32[32,1,4,2176]{3,2,1,0:T(4,128)}), f32[32,1,4,2176]{3,2,1,0:T(4,128)S(1)}, u32[]{:S(2)}, u32[]{:S(2)}) async-start(f32[32,1,4,2176]{3,2,1,0:T(4,128)} %pad_maximum_fusion), calls=%async_computation | async-start | bytes 2228224 | tf_op jit(solution)/shard_map/all_to_all | solution.py:91
  172.2 28.5 %all-to-all-done = f32[32,1,4,2176]{3,2,1,0:T(4,128)S(1)} async-done(((f32[32,1,4,2176]{3,2,1,0:T(4,128)}), f32[32,1,4,2176]{3,2,1,0:T(4,128)S(1)}, u32[]{:S(2)}, u32[]{:S(2)}) %all-to-all-start) | async-done | bytes 1114144 | tf_op jit(solution)/shard_map/all_to_all | solution.py:91
  200.8 1.2 slice.45
  202.0 1.6 reshape.463
  205.0 4.0 %all-to-all-start.1 = ((f32[8,4,2176]{2,1,0:T(4,128)}), f32[8,4,2176]{2,1,0:T(4,128)S(1)}, u32[]{:S(2)}, u32[]{:S(2)}) async-start(f32[8,4,2176]{2,1,0:T(4,128)} %copy.96), calls=%async_computation.1 | async-start | bytes 557056 | tf_op jit(solution)/shard_map/all_to_all | solution.py:119
  209.3 5.8 %all-to-all-done.1 = f32[8,4,2176]{2,1,0:T(4,128)S(1)} async-done(((f32[8,4,2176]{2,1,0:T(4,128)}), f32[8,4,2176]{2,1,0:T(4,128)S(1)}, u32[]{:S(2)}, u32[]{:S(2)}) %all-to-all-start.1) | async-done | bytes 278560 | tf_op jit(solution)/shard_map/all_to_all | solution.py:119
  216.6 9.1 %all-to-all-start.2 = ((bf16[256,4,128]{2,1,0:T(4,128)(2,1)}), bf16[256,4,128]{2,1,0:T(4,128)(2,1)S(1)}, u32[]{:S(2)}, u32[]{:S(2)}) async-start(bf16[256,4,128]{2,1,0:T(4,128)(2,1)} %broadcast_in_dim.59), calls=%async_computation.2 | async-start | bytes 524288 | tf_op jit(solution)/shard_map/all_to_all | solution.py:129
  226.6 14.8 %all-to-all-done.2 = bf16[256,4,128]{2,1,0:T(4,128)(2,1)S(1)} async-done(((bf16[256,4,128]{2,1,0:T(4,128)(2,1)}), bf16[256,4,128]{2,1,0:T(4,128)(2,1)S(1)}, u32[]{:S(2)}, u32[]{:S(2)}) %all-to-all-start.2) | async-done | bytes 262176 | tf_op jit(solution)/shard_map/all_to_all | solution.py:129
  241.4 1.9 fusion.19
  (83 shorter events, 13.6 us)
Async XLA Ops:
  7.2 124.7 %copy-start = (bf16[1,2048,384]{2,1,0:T(8,128)(2,1)S(1)}, bf16[1,2048,384]{2,1,0:T(8,128)(2,1)}, u32[]{:S(2)}) copy-start(bf16[1,2048,384]{2,1,0:T(8,128)(2,1)} %param.15) | copy-start | bytes 4718596
  7.2 2.5 copy-start.7
  7.2 3.0 %copy-start.8 = (bf16[4,2048]{1,0:T(4,128)(2,1)S(1)}, bf16[4,2048]{1,0:T(4,128)(2,1)}, u32[]{:S(2)}) copy-start(bf16[4,2048]{1,0:T(4,128)(2,1)} %param.11) | copy-start | bytes 49156
  7.2 3.0 %copy-start.9 = (bf16[4,2048]{1,0:T(4,128)(2,1)S(1)}, bf16[4,2048]{1,0:T(4,128)(2,1)}, u32[]{:S(2)}) copy-start(bf16[4,2048]{1,0:T(4,128)(2,1)} %param.10) | copy-start | bytes 49156
  7.2 112.9 %all-gather.3.cloned.1.call-start = ((), (), s32[]{:S(2)}) async-start(), calls=%async_computation.3 | async-start | bytes 8921088 | tf_op jit(solution)/shard_map/all_gather | solution.py:76
  9.6 115.2 %copy-start.2 = (bf16[1,2048,384]{2,1,0:T(8,128)(2,1)S(1)}, bf16[1,2048,384]{2,1,0:T(8,128)(2,1)}, u32[]{:S(2)}) copy-start(bf16[1,2048,384]{2,1,0:T(8,128)(2,1)} %param.16) | copy-start | bytes 4718596
  141.6 2.4 copy-start.4
  154.3 1.7 copy-start.3
  156.7 1.3 copy-start.6
  160.5 10.4 %slice-start = ((bf16[1024,4224]{1,0:T(8,128)(2,1)}), bf16[1024,128]{1,0:T(8,128)(2,1)S(1)}, s32[]{:S(2)}) async-start(bf16[1024,4224]{1,0:T(8,128)(2,1)} %all-gather.3.cloned.1.call-done), calls=%async_computation.4 | async-start | bytes 524288 | tf_op jit(solution)/shard_map/slice | solution.py:79
  160.5 40.2 %all-to-all-start = ((f32[32,1,4,2176]{3,2,1,0:T(4,128)}), f32[32,1,4,2176]{3,2,1,0:T(4,128)S(1)}, u32[]{:S(2)}, u32[]{:S(2)}) async-start(f32[32,1,4,2176]{3,2,1,0:T(4,128)} %pad_maximum_fusion), calls=%async_computation | async-start | bytes 2228224 | tf_op jit(solution)/shard_map/all_to_all | solution.py:91
  203.6 5.4 %copy-start.1 = (f32[4,128]{1,0:T(4,128)S(1)}, f32[4,128]{1,0:T(4,128)}, u32[]{:S(2)}) copy-start(f32[4,128]{1,0:T(4,128)} %param.12) | copy-start | bytes 6148
  204.1 21.6 %copy-start.5 = (bf16[2048,128]{1,0:T(8,128)(2,1)S(1)}, bf16[2048,128]{1,0:T(8,128)(2,1)}, u32[]{:S(2)}) copy-start(bf16[2048,128]{1,0:T(8,128)(2,1)} %param.14) | copy-start | bytes 1572868
  205.0 10.2 %all-to-all-start.1 = ((f32[8,4,2176]{2,1,0:T(4,128)}), f32[8,4,2176]{2,1,0:T(4,128)S(1)}, u32[]{:S(2)}, u32[]{:S(2)}) async-start(f32[8,4,2176]{2,1,0:T(4,128)} %copy.96), calls=%async_computation.1 | async-start | bytes 557056 | tf_op jit(solution)/shard_map/all_to_all | solution.py:119
  216.6 24.8 %all-to-all-start.2 = ((bf16[256,4,128]{2,1,0:T(4,128)(2,1)}), bf16[256,4,128]{2,1,0:T(4,128)(2,1)S(1)}, u32[]{:S(2)}, u32[]{:S(2)}) async-start(bf16[256,4,128]{2,1,0:T(4,128)(2,1)} %broadcast_in_dim.59), calls=%async_computation.2 | async-start | bytes 524288 | tf_op jit(solution)/shard_map/all_to_all | solution.py:129
Sparse Core Ops, SparseCore 0:
  35.2 84.8 all-gather.2
where the time goes:
time: 251 us; the launch traced here: 250 us
  waiting for transfers between devices  134 us (53%)
  blocking collectives  24.1 us (10%)
  starting transfers between devices  23.6 us (9%)
  matrix products  23.5 us (9%)
  local copies, waits for them, and re-layouts  23.4 us (9%)
  between operations  14.4 us (6%)
  other arithmetic  7.08 us (3%)
    all_gather x1, waiting for transfers between devices, on_device(): lax.all_gather(lax.all_gather(packed, 'hid', axis=0, tiled=True), 'exp',...  85 us
    all_to_all x1, waiting for transfers between devices, on_device(): lax.all_to_all(sent, 'exp', split_axis=0, concat_axis=0, tiled=True)  28.5 us
    all_gather x1, blocking collectives, on_device(): lax.all_gather(packed, 'hid', axis=0, tiled=True)  24.1 us
    all_to_all x1, waiting for transfers between devices, on_device(): lax.all_to_all(jnp.broadcast_to(logit_grad[None], (devices,) + logit_grad...  14.8 us
    all_to_all x1, starting transfers between devices, on_device(): lax.all_to_all(sent, 'exp', split_axis=0, concat_axis=0, tiled=True)  10.4 us
    all_to_all x1, starting transfers between devices, on_device(): lax.all_to_all(jnp.broadcast_to(logit_grad[None], (devices,) + logit_grad...  9.1 us
    another operation x3, local copies, waits for them, and re-layouts, sparse_terms(): take = lambda a: jnp.take_along_axis(a, rows[:, :, None], axis=1)  6.86 us
    dot_general x1, matrix products, dense_terms(): jnp.einsum('td,ufd->utf', g_rows, w_down, preferred_element_type=jnp.floa...  6.17 us
  transfers between devices with their start and end apart: 4, of which 4 were waited for; matrix products, arithmetic and copies ran while one was open for 1% of the time, Pallas kernels for 0%

commit v1 on v0

--- a/solution.py
+++ b/solution.py
@@ -2,6 +2,13 @@
 import jax.numpy as jnp
 from jax import lax
 from jax.sharding import PartitionSpec as P
+
+
+def all_by_exchange(block, axis, d):
+    size = lax.axis_size(axis)
+    blocks = jnp.stack([block for _ in range(size)])
+    blocks = lax.all_to_all(blocks, axis, split_axis=0, concat_axis=0)
+    return jnp.concatenate(blocks, axis=d)
 
 
 def softmax_rows(values):
@@ -73,9 +80,7 @@
     unit_pick = (expert_ids[:, None] == unit_expert[None, :]).astype(jnp.bfloat16)
     combine = combine_table(router_logits, selected, expert_count)
     packed = jnp.concatenate([tokens, grad_out, combine], axis=1)
-    gathered = lax.all_gather(
-        lax.all_gather(packed, "hid", axis=0, tiled=True), "exp", axis=0, tiled=True
-    )
+    gathered = all_by_exchange(lax.all_gather(packed, "hid", axis=0, tiled=True), "exp", 0)
     combine_all = gathered[:, 2 * model_width :]
     score_part, gate_pre, up_pre, back_grad = dense_terms(
         gathered[:, :model_width], gathered[:, model_width : 2 * model_width], w_gate, w_up, w_down

time: 251 us -> 360 us (1.43)
  waiting for transfers between devices: 134 us -> 236 us
  starting transfers between devices: 23.6 us -> 39.8 us
  between operations: 14.4 us -> 0.98 us
    all_to_all x0 -> x1, waiting for transfers between devices: none -> 191 us  [all_by_exchange(): blocks = lax.all_to_all(blocks, axis, split_axis=0, concat_axis=0)]
    all_gather x1 -> x0, waiting for transfers between devices: 85 us -> none  [on_device(): lax.all_gather(lax.all_gather(packed, 'hid', axis=0, tiled=True), 'exp',...]
    all_to_all x0 -> x1, starting transfers between devices: none -> 17.2 us  [all_by_exchange(): blocks = lax.all_to_all(blocks, axis, split_axis=0, concat_axis=0)]
    all_to_all x1, starting transfers between devices: 10.4 us -> 5.66 us  [on_device(): lax.all_to_all(sent, 'exp', split_axis=0, concat_axis=0, tiled=True)]
    all_to_all x1, waiting for transfers between devices: 28.5 us -> 24.4 us  [on_device(): lax.all_to_all(sent, 'exp', split_axis=0, concat_axis=0, tiled=True)]
    all_to_all x1, starting transfers between devices: 4.05 us -> 7.96 us  [on_device(): lax.all_to_all(hid_sent, 'hid', split_axis=0, concat_axis=0, tiled=True)]
    another operation x0 -> x1, local copies, waits for them, and re-layouts: none -> 3.88 us  [all_by_exchange(): blocks = jnp.stack([block for _ in range(size)])]
where the time goes in v1:
time: 360 us; the launch traced here: 359 us
  waiting for transfers between devices  236 us (66%)
  starting transfers between devices  39.8 us (11%)
  local copies, waits for them, and re-layouts  26.1 us (7%)
  matrix products  24.2 us (7%)
  blocking collectives  24.1 us (7%)
  other arithmetic  7.74 us (2%)
    all_to_all x1, waiting for transfers between devices, all_by_exchange(): blocks = lax.all_to_all(blocks, axis, split_axis=0, concat_axis=0)  191 us
    all_to_all x1, waiting for transfers between devices, on_device(): lax.all_to_all(sent, 'exp', split_axis=0, concat_axis=0, tiled=True)  24.4 us
    all_gather x1, blocking collectives, on_device(): lax.all_gather(packed, 'hid', axis=0, tiled=True)  24.1 us
    all_to_all x1, starting transfers between devices, all_by_exchange(): blocks = lax.all_to_all(blocks, axis, split_axis=0, concat_axis=0)  17.2 us
    all_to_all x1, waiting for transfers between devices, on_device(): lax.all_to_all(jnp.broadcast_to(logit_grad[None], (devices,) + logit_grad...  14.8 us
    all_to_all x1, starting transfers between devices, on_device(): lax.all_to_all(jnp.broadcast_to(logit_grad[None], (devices,) + logit_grad...  8.95 us
    all_to_all x1, starting transfers between devices, on_device(): lax.all_to_all(hid_sent, 'hid', split_axis=0, concat_axis=0, tiled=True)  7.96 us
  transfers between devices with their start and end apart: 4, of which 4 were waited for; matrix products, arithmetic and copies ran while one was open for 1% of the time, Pallas kernels for 0%

profile of v1, /device:TPU:1, one launch (start us, length us, event | category | flops | bytes accessed | tf_op | source)
XLA Modules:
  0.0 359.1 jit_solution(4121491500593864533)
XLA Ops:
  1.6 1.4 gather_fusion.1
  3.6 24.1 %all-gather = bf16[8,4,4224]{2,1,0:T(4,128)(2,1)S(1)} all-gather(bf16[1,4,4224]{2,1,0:T(4,128)(2,1)S(1)} %maximum_bitcast_fusion), channel_id=1, replica_groups=mesh['exp'=32,'hid'=8] {'hid'}, dimensions={0}, use_global_device_ids=true | all-gather | bytes 304128 | tf_op jit(solution)/shard_map/all_gather | solution.py:83
  27.8 3.9 %stack.2 = bf16[32,32,4224]{2,1,0:T(8,128)(2,1)} broadcast(bf16[32,4224]{1,0:T(8,128)(2,1)S(1)} %reshape.451), dimensions={1,2} | broadcast | bytes 8921088 | tf_op jit(solution)/shard_map/stack | solution.py:9
  31.7 17.2 %all-to-all-start = ((bf16[32,32,4224]{2,1,0:T(8,128)(2,1)}), bf16[32,32,4224]{2,1,0:T(8,128)(2,1)}, u32[]{:S(2)}, u32[]{:S(2)}) async-start(bf16[32,32,4224]{2,1,0:T(8,128)(2,1)} %stack.2), calls=%async_computation | async-start | bytes 17301504 | tf_op jit(solution)/shard_map/all_to_all | solution.py:10
  49.0 191.1 %all-to-all-done = bf16[32,32,4224]{2,1,0:T(8,128)(2,1)} async-done(((bf16[32,32,4224]{2,1,0:T(8,128)(2,1)}), bf16[32,32,4224]{2,1,0:T(8,128)(2,1)}, u32[]{:S(2)}, u32[]{:S(2)}) %all-to-all-start) | async-done | bytes 8650784 | tf_op jit(solution)/shard_map/all_to_all | solution.py:10
  243.9 5.3 %fusion.4 = f32[1024,384]{0,1:T(8,128)} fusion(bf16[1024,4224]{1,0:T(8,128)(2,1)} %bitcast.2, bf16[1,2048,384]{2,1,0:T(8,128)(2,1)S(1)} %copy-done.2), kind=kOutput, calls=%fused_computation.9 | convolution fusion | flops 1610612736 | bytes 7340032 | tf_op jit(solution)/shard_map/td,udf->utf/dot_general | solution.py:40
  249.1 5.3 %fusion.2 = f32[1024,384]{0,1:T(8,128)} fusion(bf16[1024,4224]{1,0:T(8,128)(2,1)} %bitcast.2, bf16[1,2048,384]{2,1,0:T(8,128)(2,1)S(1)} %copy-done), kind=kOutput, calls=%fused_computation.7 | convolution fusion | flops 1610612736 | bytes 7340032 | tf_op jit(solution)/shard_map/td,udf->utf/dot_general | solution.py:39
  254.4 1.7 copy.90
  256.1 1.9 copy.91
  258.0 6.7 %fusion.7 = (f32[1024]{0:T(1024)S(1)}, f32[1024,384]{0,1:T(8,128)}) fusion(f32[1024,384]{0,1:T(8,128)} %fusion.4, f32[1024,384]{0,1:T(8,128)} %fusion.2, bf16[1,384,2048]{2,1,0:T(8,128)(2,1)} %param.17, bf16[1024,4224]{1,0:T(8,128)(2,1)} %bitcast.2), kind=kOutput, calls=%fused_computation.15 | convolution fusion | flops 1613364224 | bytes 10489856 | tf_op jit(solution)/shard_map/td,ufd->utf/dot_general | solution.py:41
  265.5 2.9 gather_fusion.3
  269.1 1.9 copy.89
  274.1 1.8 fusion.11
  276.6 1.3 transpose_reshape.6
  277.9 2.6 pad_maximum_fusion
  280.4 5.7 %all-to-all-start.1 = ((f32[32,1,4,2176]{3,2,1,0:T(4,128)}), f32[32,1,4,2176]{3,2,1,0:T(4,128)S(1)}, u32[]{:S(2)}, u32[]{:S(2)}) async-start(f32[32,1,4,2176]{3,2,1,0:T(4,128)} %pad_maximum_fusion), calls=%async_computation.1 | async-start | bytes 2228224 | tf_op jit(solution)/shard_map/all_to_all | solution.py:96
  288.4 24.4 %all-to-all-done.1 = f32[32,1,4,2176]{3,2,1,0:T(4,128)S(1)} async-done(((f32[32,1,4,2176]{3,2,1,0:T(4,128)}), f32[32,1,4,2176]{3,2,1,0:T(4,128)S(1)}, u32[]{:S(2)}, u32[]{:S(2)}) %all-to-all-start.1) | async-done | bytes 1114144 | tf_op jit(solution)/shard_map/all_to_all | solution.py:96
  312.9 1.2 slice.45
  314.1 1.6 reshape.469
  317.0 8.0 %all-to-all-start.2 = ((f32[8,4,2176]{2,1,0:T(4,128)}), f32[8,4,2176]{2,1,0:T(4,128)S(1)}, u32[]{:S(2)}, u32[]{:S(2)}) async-start(f32[8,4,2176]{2,1,0:T(4,128)} %copy.96), calls=%async_computation.2 | async-start | bytes 557056 | tf_op jit(solution)/shard_map/all_to_all | solution.py:124
  325.3 5.8 %all-to-all-done.2 = f32[8,4,2176]{2,1,0:T(4,128)S(1)} async-done(((f32[8,4,2176]{2,1,0:T(4,128)}), f32[8,4,2176]{2,1,0:T(4,128)S(1)}, u32[]{:S(2)}, u32[]{:S(2)}) %all-to-all-start.2) | async-done | bytes 278560 | tf_op jit(solution)/shard_map/all_to_all | solution.py:124
  332.6 8.9 %all-to-all-start.3 = ((bf16[256,4,128]{2,1,0:T(4,128)(2,1)}), bf16[256,4,128]{2,1,0:T(4,128)(2,1)S(1)}, u32[]{:S(2)}, u32[]{:S(2)}) async-start(bf16[256,4,128]{2,1,0:T(4,128)(2,1)} %broadcast_in_dim.59), calls=%async_computation.3 | async-start | bytes 524288 | tf_op jit(solution)/shard_map/all_to_all | solution.py:134
  342.5 14.8 %all-to-all-done.3 = bf16[256,4,128]{2,1,0:T(4,128)(2,1)S(1)} async-done(((bf16[256,4,128]{2,1,0:T(4,128)(2,1)}), bf16[256,4,128]{2,1,0:T(4,128)(2,1)S(1)}, u32[]{:S(2)}, u32[]{:S(2)}) %all-to-all-start.3) | async-done | bytes 262176 | tf_op jit(solution)/shard_map/all_to_all | solution.py:134
  357.2 1.9 fusion.19
  (86 shorter events, 16.8 us)
Async XLA Ops:
  0.6 248.5 %copy-start = (bf16[1,2048,384]{2,1,0:T(8,128)(2,1)S(1)}, bf16[1,2048,384]{2,1,0:T(8,128)(2,1)}, u32[]{:S(2)}) copy-start(bf16[1,2048,384]{2,1,0:T(8,128)(2,1)} %param.15) | copy-start | bytes 4718596
  0.6 2.4 copy-start.7
  0.7 2.9 copy-start.8
  0.7 2.9 copy-start.9
  31.7 212.2 %copy-start.2 = (bf16[1,2048,384]{2,1,0:T(8,128)(2,1)S(1)}, bf16[1,2048,384]{2,1,0:T(8,128)(2,1)}, u32[]{:S(2)}) copy-start(bf16[1,2048,384]{2,1,0:T(8,128)(2,1)} %param.16) | copy-start | bytes 4718596
  31.7 208.4 %all-to-all-start = ((bf16[32,32,4224]{2,1,0:T(8,128)(2,1)}), bf16[32,32,4224]{2,1,0:T(8,128)(2,1)}, u32[]{:S(2)}, u32[]{:S(2)}) async-start(bf16[32,32,4224]{2,1,0:T(8,128)(2,1)} %stack.2), calls=%async_computation | async-start | bytes 17301504 | tf_op jit(solution)/shard_map/all_to_all | solution.py:10
  49.0 192.5 %copy-start.10 = (s32[32]{0:T(128)}, s32[32]{0:T(128)S(1)}, u32[]{:S(2)}) copy-start(s32[32]{0:T(128)S(1)} %get-tuple-element.18) | copy-start | bytes 388
  249.1 5.3 %copy-start.4 = (f32[1024,384]{0,1:T(8,128)S(1)}, f32[1024,384]{0,1:T(8,128)}, u32[]{:S(2)}) copy-start(f32[1024,384]{0,1:T(8,128)} %fusion.4) | copy-start | bytes 4718596
  274.1 1.8 copy-start.3
  276.6 1.3 copy-start.6
  280.4 6.7 %copy-start.11 = (s32[32]{0:T(128)S(1)}, s32[32]{0:T(128)}, u32[]{:S(2)}) copy-start(s32[32]{0:T(128)} %copy-done.10) | copy-start | bytes 388
  280.4 32.4 %all-to-all-start.1 = ((f32[32,1,4,2176]{3,2,1,0:T(4,128)}), f32[32,1,4,2176]{3,2,1,0:T(4,128)S(1)}, u32[]{:S(2)}, u32[]{:S(2)}) async-start(f32[32,1,4,2176]{3,2,1,0:T(4,128)} %pad_maximum_fusion), calls=%async_computation.1 | async-start | bytes 2228224 | tf_op jit(solution)/shard_map/all_to_all | solution.py:96
  315.7 9.3 %copy-start.1 = (f32[4,128]{1,0:T(4,128)S(1)}, f32[4,128]{1,0:T(4,128)}, u32[]{:S(2)}) copy-start(f32[4,128]{1,0:T(4,128)} %param.12) | copy-start | bytes 6148
  316.2 25.4 %copy-start.5 = (bf16[2048,128]{1,0:T(8,128)(2,1)S(1)}, bf16[2048,128]{1,0:T(8,128)(2,1)}, u32[]{:S(2)}) copy-start(bf16[2048,128]{1,0:T(8,128)(2,1)} %param.14) | copy-start | bytes 1572868
  317.0 14.1 %all-to-all-start.2 = ((f32[8,4,2176]{2,1,0:T(4,128)}), f32[8,4,2176]{2,1,0:T(4,128)S(1)}, u32[]{:S(2)}, u32[]{:S(2)}) async-start(f32[8,4,2176]{2,1,0:T(4,128)} %copy.96), calls=%async_computation.2 | async-start | bytes 557056 | tf_op jit(solution)/shard_map/all_to_all | solution.py:124
  332.6 24.7 %all-to-all-start.3 = ((bf16[256,4,128]{2,1,0:T(4,128)(2,1)}), bf16[256,4,128]{2,1,0:T(4,128)(2,1)S(1)}, u32[]{:S(2)}, u32[]{:S(2)}) async-start(bf16[256,4,128]{2,1,0:T(4,128)(2,1)} %broadcast_in_dim.59), calls=%async_computation.3 | async-start | bytes 524288 | tf_op jit(solution)/shard_map/all_to_all | solution.py:134
